TPU v7x, 32 devices: a whole 2x2x4 slice. The times are simulated.
32 devices in a mesh: replica: 2 (over y), tp: 4 (over x, core), dp: 4 (over z).
Axes of the slice: x: 2, y: 2, z: 4, core: 2. Of those that a mesh axis runs over, the one named last changes fastest.
Arguments:
- tokens: bfloat16 [8192, 8192], P(('replica', 'dp'), 'tp'), parts along dimension 0, may hold values from -6 to 6
- query_weight: bfloat16 [8192, 4096], P(None, 'tp'), may hold values from -0.0625 to 0.0625
- value_weight: bfloat16 [8192, 1024], P(None, 'tp'), may hold values from -0.0625 to 0.0625
- adapter_down_factors: bfloat16 [256, 8192, 128], P('dp', 'tp'), may hold values from -0.0625 to 0.0625
- query_up_factors: bfloat16 [256, 64, 4096], P('dp', None, 'tp'), may hold values from -0.75 to 0.75
- value_up_factors: bfloat16 [256, 64, 1024], P('dp', None, 'tp'), may hold values from -0.75 to 0.75
- request_adapter: int32 [32], P('replica'), parts along dimension 0, may hold values from 0 to 255
- lengths: int32 [32], P('replica'), parts along dimension 0, may hold values from 1 to 1024, 4096 in all
- home: int32 [256], replicated, may hold values from 0 to 255, each once
Outputs:
- query: bfloat16 [8192, 4096], P(('replica', 'dp'), 'tp'), parts along dimension 0
- value: bfloat16 [8192, 1024], P(('replica', 'dp'), 'tp'), parts along dimension 0
There are 2 independent parts, one for each index of `replica`. A program takes and returns all parts, laid end to end along the dimension named above; an argument that names none is the same for every part. Nothing has to cross between parts.
Inputs may be any that keep to these rules, and one draw needn't show every extreme that they name: The lengths sum to 4096; the requests lie one after another in the token order. `home`: each of 0 to 255 appears once.
All inputs are finite; a program needn't handle non-finite values.
Results may differ from a plain program's by a relative error of at most 0.0031.
Values may be sent and summed in bfloat16 or wider, within the bound.
No kernel may reach another device: no remote copies, remote signals or barrier semaphores. Data moves between devices by JAX's collectives and lax.ppermute only.
A program may use at most 192 MiB of HBM per device.

v0:
```python
import jax
import jax.numpy as jnp
from jax import lax
from jax.sharding import PartitionSpec as P

adapter_scale = 0.5


def owners(lengths, first_row, count):
    starts = jnp.cumsum(lengths, dtype=jnp.int32) - lengths
    rows_here = first_row + jnp.arange(count, dtype=jnp.int32)
    return (
        jnp.sum((rows_here[:, None] >= starts[None, :]).astype(jnp.int32), axis=1, dtype=jnp.int32)
        - 1
    )


def body(
    tokens,
    query_weight,
    value_weight,
    adapter_down_factors,
    query_up_factors,
    value_up_factors,
    request_adapter,
    lengths,
    home,
):
    tok_rows = tokens.shape[0]
    stored_adapters = adapter_down_factors.shape[0]
    rank_extent = query_up_factors.shape[1]
    dp_index = lax.axis_index("dp")
    adapter_slots = home[request_adapter]
    holder = adapter_slots // stored_adapters
    location = adapter_slots % stored_adapters
    mine = holder == dp_index

    def select_rows(table):
        taken = jnp.take(table, location, axis=0)
        return jnp.where(mine[:, None, None], taken, jnp.zeros_like(taken))

    summed = (
        lax.psum(select_rows(adapter_down_factors), "dp").astype(jnp.float32),
        lax.psum(select_rows(query_up_factors), "dp").astype(jnp.float32),
        lax.psum(select_rows(value_up_factors), "dp").astype(jnp.float32),
    )
    down_f = summed[0].astype(jnp.bfloat16)
    up_q = summed[1].astype(jnp.bfloat16)
    up_v = summed[2].astype(jnp.bfloat16)
    owner = owners(lengths, dp_index * tok_rows, tok_rows)
    first_req = owner[0]
    last_req = owner[tok_rows - 1] + 1
    zero_q = jnp.zeros((tok_rows, query_weight.shape[1]), jnp.float32)
    zero_v = jnp.zeros((tok_rows, value_weight.shape[1]), jnp.float32)
    piece = lax.all_gather(tokens, "tp", axis=1, tiled=True)
    query_plain = jnp.dot(piece, query_weight, preferred_element_type=jnp.float32)
    value_plain = jnp.dot(piece, value_weight, preferred_element_type=jnp.float32)

    def down_group(request_number, total):
        factor = lax.dynamic_index_in_dim(down_f, request_number, 0, keepdims=False)
        product = jnp.dot(tokens, factor, preferred_element_type=jnp.float32)
        return total + jnp.where((owner == request_number)[:, None], product, 0.0)

    selected = lax.fori_loop(
        first_req, last_req, down_group, jnp.zeros((tok_rows, down_f.shape[2]), jnp.float32)
    )
    down = lax.psum(selected, "tp").astype(jnp.bfloat16)
    down_q = down[:, :rank_extent]
    down_v = down[:, rank_extent:]

    def up_group(request_number, totals):
        factor_q = lax.dynamic_index_in_dim(up_q, request_number, 0, keepdims=False)
        factor_v = lax.dynamic_index_in_dim(up_v, request_number, 0, keepdims=False)
        inside = (owner == request_number)[:, None]
        part_q = jnp.dot(down_q, factor_q, preferred_element_type=jnp.float32)
        part_v = jnp.dot(down_v, factor_v, preferred_element_type=jnp.float32)
        return (
            totals[0] + jnp.where(inside, part_q, 0.0),
            totals[1] + jnp.where(inside, part_v, 0.0),
        )

    query_lowrank, value_lowrank = lax.fori_loop(first_req, last_req, up_group, (zero_q, zero_v))
    query = (query_plain + adapter_scale * query_lowrank).astype(jnp.bfloat16)
    value = (value_plain + adapter_scale * value_lowrank).astype(jnp.bfloat16)
    return (query, value)


def solution(mesh):
    in_specs = (
        P(("replica", "dp"), "tp"),
        P(None, "tp"),
        P(None, "tp"),
        P("dp", "tp", None),
        P("dp", None, "tp"),
        P("dp", None, "tp"),
        P("replica"),
        P("replica"),
        P(),
    )
    out_specs = (P(("replica", "dp"), "tp"), P(("replica", "dp"), "tp"))
    return jax.shard_map(body, mesh=mesh, in_specs=in_specs, out_specs=out_specs, check_vma=False)
```

profile of v0, /device:TPU:20, one launch (start us, length us, event | category | flops | bytes accessed | tf_op | source)
XLA Modules:
  0.0 585.5 jit_solution(7345490909103174528)
XLA Ops:
  8.1 0.8 compare_select_fusion.2
  8.9 1.3 gather_fusion
  10.3 7.3 %gather_fusion.2 = bf16[16,2048,128]{2,1,0:T(8,128)(2,1)} fusion(bf16[64,2048,128]{2,1,0:T(8,128)(2,1)} %param.16, s32[1024]{0:T(1024)S(1)} %pad_clamp_fusion), kind=kCustom, calls=%fused_computation.2 | custom fusion | bytes 16777280 | tf_op jit(solution)/shard_map/jit(_take)/gather | solution.py:39
  17.6 5.4 gather_fusion.1
  22.9 7.7 %select_select_fusion = bf16[16,2048,128]{2,1,0:T(8,128)(2,1)} fusion(bf16[16,2048,128]{2,1,0:T(8,128)(2,1)} %gather_fusion.2, pred[16]{0:T(512)(128)(4,1)S(1)} %get-tuple-element.125, pred[16]{0:T(512)(128)(4,1)S(1)} %get-tuple-element.124), kind=kLoop, calls=%fused_computation.22 | loop fusion | flops 8388608 | bytes 16777248 | tf_op jit(solution)/shard_map/jit(_where)/select_n | solution.py:40
  30.7 1.6 select_select_fusion.1
  32.3 0.6 gather_fusion.3
  32.9 0.9 select_select_fusion.2
  34.8 0.6 fusion.18
  36.6 372.7 %all-reduce.4.cloned.1.call-done = (bf16[16,64,1024]{2,1,0:T(8,128)(2,1)}, bf16[16,2048,128]{2,1,0:T(8,128)(2,1)}, bf16[16,64,256]{2,1,0:T(8,128)(2,1)}) async-done(((bf16[16,64,1024]{2,1,0:T(8,128)(2,1)}, bf16[16,2048,128]{2,1,0:T(8,128)(2,1)}, bf16[16,64,256]{2,1,0:T(8,128)(2,1)}), (bf16[16,64,1024]{2,1,0:T(8,128)(2,1)}, bf16[16,2048,128]{2,1,0:T(8,128)(2,1)}, ...) | async-done | bytes 11010064 | tf_op jit(solution)/shard_map/psum | solution.py:44
  409.4 31.9 %while.22 = (s32[]{:T(128)}, f32[1024,128]{0,1:T(8,128)S(1)}, s32[]{:T(128)}, s32[1024]{0:T(1024)S(1)}, bf16[16,2048,128]{2,1,0:T(8,128)(2,1)}, /*index=5*/bf16[...) while((s32[]{:T(128)}, f32[1024,128]{0,1:T(8,128)S(1)}, s32[]{:T(128)}, s32[1024]{0:T(1024)S(1)}, ...), condition=%wide.region_6.7_spmd, body=%wide.region_5.6_spmd.sunk | while | flops 537134080 | bytes 5773447 | solution.py:64
  409.5 3.9 fusion.36
  413.5 3.9 fusion.36
  417.4 3.9 fusion.36
  421.4 3.9 fusion.36
  425.4 3.9 fusion.36
  429.4 3.9 fusion.36
  433.4 3.9 fusion.36
  437.4 3.9 fusion.36
  441.6 16.9 %all-reduce.5 = bf16[1024,128]{1,0:T(8,128)(2,1)S(1)} all-reduce(f32[1024,128]{1,0:T(8,128)S(1)} %copy.20), channel_id=1, replica_groups=mesh['replica'=2,'tp'=4,'dp'=4] {'tp'}, use_global_device_ids=true, to_apply=%region_7.8 | all-reduce | flops 131072 | bytes 786432 | tf_op jit(solution)/shard_map/psum | solution.py:67
  458.6 2.5 broadcast_in_dim.118
  461.2 81.0 %while.23 = (s32[]{:T(128)}, f32[1024,1024]{0,1:T(8,128)}, f32[1024,256]{0,1:T(8,128)S(1)}, s32[]{:T(128)}, s32[1024]{0:T(1024)S(1)}, /*index=5*/bf16[16,64,1024...) while((s32[]{:T(128)}, f32[1024,1024]{0,1:T(8,128)}, ...), condition=%wide.region_9.10_spmd, body=%wide.region_8.9_spmd.sunk | while | flops 170394624 | bytes 10919075 | solution.py:82
  463.5 0.6 broadcast_compare_fusion.5
  464.0 5.0 bitcast_add_fusion.2
  469.0 1.1 fusion.41
  473.5 0.6 broadcast_compare_fusion.5
  474.1 5.0 bitcast_add_fusion.2
  479.0 1.1 fusion.41
  483.5 0.6 broadcast_compare_fusion.5
  484.1 5.0 bitcast_add_fusion.2
  489.1 1.1 fusion.41
  494.1 5.0 bitcast_add_fusion.2
  499.1 1.1 fusion.41
  503.6 0.6 broadcast_compare_fusion.5
  504.2 5.0 bitcast_add_fusion.2
  509.1 1.1 fusion.41
  513.6 0.6 broadcast_compare_fusion.5
  514.2 5.0 bitcast_add_fusion.2
  519.2 1.1 fusion.41
  523.6 0.6 broadcast_compare_fusion.5
  524.2 5.0 bitcast_add_fusion.2
  529.2 1.1 fusion.41
  533.7 0.6 broadcast_compare_fusion.5
  534.3 5.0 bitcast_add_fusion.2
  539.2 1.1 fusion.41
  542.2 5.4 copy.21
  547.9 24.8 %add_convert_fusion = bf16[1024,1024]{1,0:T(8,128)(2,1)} fusion(f32[1024,1024]{1,0:T(8,128)} %copy.21, bf16[1024,8192]{1,0:T(8,128)(2,1)} %all-gather.2.cloned.1.call-done, bf16[8192,1024]{1,0:T(8,128)(2,1)} %param.14), kind=kOutput, calls=%fused_computation.23 | convolution fusion | flops 17183014912 | bytes 39845888 | tf_op jit(solution)/shard_map/dot_general | solution.py:56
  572.8 5.3 fusion.13
  (42 shorter events, 2.5 us)
Async XLA Ops:
  8.0 24.3 %copy-start = (bf16[64,64,256]{2,1,0:T(8,128)(2,1)S(1)}, bf16[64,64,256]{2,1,0:T(8,128)(2,1)}, u32[]{:S(2)}) copy-start(bf16[64,64,256]{2,1,0:T(8,128)(2,1)} %param.18) | copy-start | bytes 6291460
  8.0 401.4 %all-reduce.4.cloned.1.call-start = ((), (), s32[]{:S(2)}) async-start(), calls=%async_computation.1 | async-start | bytes 22020096 | tf_op jit(solution)/shard_map/psum | solution.py:44
  22.9 7.7 %copy-start.2 = (bf16[16,64,1024]{2,1,0:T(8,128)(2,1)S(1)}, bf16[16,64,1024]{2,1,0:T(8,128)(2,1)}, u32[]{:S(2)}) copy-start(bf16[16,64,1024]{2,1,0:T(8,128)(2,1)} %gather_fusion.1) | copy-start | bytes 6291460
  33.8 0.7 copy-start.3
  33.8 514.0 %all-gather.2.cloned.1.call-start = ((), (), s32[]{:S(2)}) async-start(), calls=%async_computation | async-start | bytes 20971520 | tf_op jit(solution)/shard_map/all_gather | solution.py:55
  547.9 24.9 %copy-start.4 = (bf16[1024,8192]{1,0:T(8,128)(2,1)S(1)}, bf16[1024,8192]{1,0:T(8,128)(2,1)}, u32[]{:S(2)}) copy-start(bf16[1024,8192]{1,0:T(8,128)(2,1)} %all-gather.2.cloned.1.call-done) | copy-start | bytes 50331652
  547.9 24.8 %copy-start.5 = (bf16[8192,256]{1,0:T(8,128)(2,1)S(1)}, bf16[8192,256]{1,0:T(8,128)(2,1)}, u32[]{:S(2)}) copy-start(bf16[8192,256]{1,0:T(8,128)(2,1)} %param.15) | copy-start | bytes 12582916
  572.8 5.3 copy-start.1
Sparse Core Ops, SparseCore 0:
  34.0 375.3 all-reduce.3
Sparse Core Ops, SparseCore 1:
  35.9 106.8 all-gather.1
where the time goes:
time: 587 us; the launch traced here: 585 us
  waiting for transfers between devices  373 us (64%)
  matrix products  110 us (19%)
  loops' own time  28.3 us (5%)
  local copies, waits for them, and re-layouts  24 us (4%)
  blocking collectives  16.9 us (3%)
  between operations  16.8 us (3%)
  other arithmetic  16 us (3%)
    psum x1, waiting for transfers between devices, body(): lax.psum(select_rows(query_up_factors), 'dp').astype(jnp.float32)  373 us
    dot_general x8, matrix products, up_group(): part_q = jnp.dot(down_q, factor_q, preferred_element_type=jnp.float32)  39.7 us
    dot_general x8, matrix products, down_group(): product = jnp.dot(tokens, factor, preferred_element_type=jnp.float32)  31.6 us
    another operation x1, loops' own time, body(): lax.fori_loop(first_req, last_req, up_group, (zero_q, zero_v))  28 us
    dot_general x1, matrix products, body(): jnp.dot(piece, query_weight, preferred_element_type=jnp.float32)  24.8 us
    psum x1, blocking collectives, body(): down = lax.psum(selected, 'tp').astype(jnp.bfloat16)  16.9 us
    gather x3, local copies, waits for them, and re-layouts, select_rows(): taken = jnp.take(table, location, axis=0)  13.3 us
  transfers between devices with their start and end apart: 2, of which 1 were waited for; matrix products, arithmetic and copies ran while one was open for 16% of the time, Pallas kernels for 0%

commit v1 on v0

--- a/solution.py
+++ b/solution.py
@@ -26,6 +26,11 @@
     lengths,
     home,
 ):
+
+    def treat_ladders(array_here, axis_name):
+        work_now = jax.lax.all_gather(array_here, axis_name)
+        return jnp.sum(work_now, axis=0)
+
     tok_rows = tokens.shape[0]
     stored_adapters = adapter_down_factors.shape[0]
     rank_extent = query_up_factors.shape[1]
@@ -41,7 +46,7 @@
 
     summed = (
         lax.psum(select_rows(adapter_down_factors), "dp").astype(jnp.float32),
-        lax.psum(select_rows(query_up_factors), "dp").astype(jnp.float32),
+        treat_ladders(select_rows(query_up_factors), "dp").astype(jnp.float32),
         lax.psum(select_rows(value_up_factors), "dp").astype(jnp.float32),
     )
     down_f = summed[0].astype(jnp.bfloat16)

time: 587 us -> 631 us (1.075)
  waiting for transfers between devices: 373 us -> 409 us
  other arithmetic: 16 us -> 23.3 us
    all_gather x0 -> x1, waiting for transfers between devices: none -> 99.6 us  [treat_ladders(): work_now = jax.lax.all_gather(array_here, axis_name)]
    psum x1, waiting for transfers between devices: 373 us -> 299 us  [body(): lax.psum(select_rows(adapter_down_factors), 'dp').astype(jnp.float32)]
    all_gather x1, waiting for transfers between devices: 0.03 us -> 10 us  [body(): piece = lax.all_gather(tokens, 'tp', axis=1, tiled=True)]
    reduce_sum x0 -> x1, other arithmetic: none -> 7.52 us  [treat_ladders(): return jnp.sum(work_now, axis=0)]
  transfers between devices with their start and end apart: 2 -> 3, of which waited for: 1 -> 3; matrix products, arithmetic and copies ran while one was open for 16% -> 17% of each run, Pallas kernels for 0% -> 0%
where the time goes in v1:
time: 631 us; the launch traced here: 628 us
  waiting for transfers between devices  409 us (65%)
  matrix products  112 us (18%)
  loops' own time  27.9 us (4%)
  other arithmetic  23.3 us (4%)
  local copies, waits for them, and re-layouts  22.9 us (4%)
  blocking collectives  17.1 us (3%)
  between operations  15.2 us (2%)
    psum x1, waiting for transfers between devices, body(): lax.psum(select_rows(adapter_down_factors), 'dp').astype(jnp.float32)  299 us
    all_gather x1, waiting for transfers between devices, treat_ladders(): work_now = jax.lax.all_gather(array_here, axis_name)  99.6 us
    dot_general x8, matrix products, up_group(): part_q = jnp.dot(down_q, factor_q, preferred_element_type=jnp.float32)  40.6 us
    dot_general x8, matrix products, down_group(): product = jnp.dot(tokens, factor, preferred_element_type=jnp.float32)  32.6 us
    another operation x1, loops' own time, body(): lax.fori_loop(first_req, last_req, up_group, (zero_q, zero_v))  27.6 us
    dot_general x1, matrix products, body(): jnp.dot(piece, query_weight, preferred_element_type=jnp.float32)  24.8 us
    psum x1, blocking collectives, body(): down = lax.psum(selected, 'tp').astype(jnp.bfloat16)  17.1 us
  transfers between devices with their start and end apart: 3, of which 3 were waited for; matrix products, arithmetic and copies ran while one was open for 17% of the time, Pallas kernels for 0%

profile of v1, /device:TPU:20, one launch (start us, length us, event | category | flops | bytes accessed | tf_op | source)
XLA Modules:
  0.0 627.9 jit_solution(869295210236498006)
XLA Ops:
  7.2 0.8 compare_select_fusion.2
  8.0 1.3 gather_fusion
  9.4 7.3 %gather_fusion.2 = bf16[16,2048,128]{2,1,0:T(8,128)(2,1)} fusion(bf16[64,2048,128]{2,1,0:T(8,128)(2,1)} %param.16, s32[1024]{0:T(1024)S(1)} %pad_clamp_fusion), kind=kCustom, calls=%fused_computation.2 | custom fusion | bytes 16777280 | tf_op jit(solution)/shard_map/jit(_take)/gather | solution.py:44
  16.7 0.6 gather_fusion.3
  17.3 7.6 %select_select_fusion = bf16[16,2048,128]{2,1,0:T(8,128)(2,1)} fusion(bf16[16,2048,128]{2,1,0:T(8,128)(2,1)} %gather_fusion.2, pred[16]{0:T(512)(128)(4,1)S(1)} %get-tuple-element.124, pred[16]{0:T(512)(128)(4,1)S(1)} %get-tuple-element.123), kind=kLoop, calls=%fused_computation.22 | loop fusion | flops 8388608 | bytes 16777248 | tf_op jit(solution)/shard_map/jit(_where)/select_n | solution.py:45
  24.9 0.9 select_select_fusion.1
  25.9 4.1 gather_fusion.1
  30.0 1.6 fusion.13
  31.7 0.7 all-gather.3.cloned.1.call-update
  32.8 0.7 fusion.19
  34.7 299.1 %all-reduce.4.cloned.1.call-done = (bf16[16,2048,128]{2,1,0:T(8,128)(2,1)}, bf16[16,64,256]{2,1,0:T(8,128)(2,1)}) async-done(((bf16[16,2048,128]{2,1,0:T(8,128)(2,1)}, bf16[16,64,256]{2,1,0:T(8,128)(2,1)}), (bf16[16,2048,128]{2,1,0:T(8,128)(2,1)}, bf16[16,64,256]{2,1,0:T(8,128)(2,1)})) %all-reduce.4.cloned.1.call-update) | async-done | bytes 8912912 | tf_op jit(solution)/shard_map/psum | solution.py:48
  333.8 32.9 %while.22 = (s32[]{:T(128)}, f32[1024,128]{0,1:T(8,128)S(1)}, s32[]{:T(128)}, s32[1024]{0:T(1024)S(1)}, bf16[16,2048,128]{2,1,0:T(8,128)(2,1)}, /*index=5*/bf16[...) while((s32[]{:T(128)}, f32[1024,128]{0,1:T(8,128)S(1)}, s32[]{:T(128)}, s32[1024]{0:T(1024)S(1)}, ...), condition=%wide.region_6.7_spmd, body=%wide.region_5.6_spmd.sunk | while | flops 537134080 | bytes 5773447 | solution.py:69
  333.9 3.9 fusion.37
  337.9 4.0 fusion.37
  341.9 4.5 fusion.37
  346.4 4.3 fusion.37
  350.8 3.9 fusion.37
  354.8 4.0 fusion.37
  358.8 3.9 fusion.37
  362.8 3.9 fusion.37
  367.0 17.1 %all-reduce.5 = bf16[1024,128]{1,0:T(8,128)(2,1)S(1)} all-reduce(f32[1024,128]{1,0:T(8,128)S(1)} %copy.24), channel_id=1, replica_groups=mesh['replica'=2,'tp'=4,'dp'=4] {'tp'}, use_global_device_ids=true, to_apply=%region_7.8 | all-reduce | flops 131072 | bytes 786432 | tf_op jit(solution)/shard_map/psum | solution.py:72
  384.2 99.6 %all-gather.5.cloned.1.call-done = bf16[4,16,64,1024]{3,2,1,0:T(8,128)(2,1)} async-done(((bf16[1,16,64,1024]{3,2,1,0:T(8,128)(2,1)}), bf16[4,16,64,1024]{3,2,1,0:T(8,128)(2,1)}) %all-gather.5.cloned.1.call-update) | async-done | bytes 8388624 | tf_op jit(solution)/shard_map/all_gather | solution.py:31
  483.8 7.5 %reduce_sum.22 = bf16[16,64,1024]{2,1,0:T(8,128)(2,1)} reduce(bf16[4,16,64,1024]{3,2,1,0:T(8,128)(2,1)} %all-gather.5.cloned.1.call-done, bf16[]{:T(256)} %constant.120.clone.1), dimensions={0}, to_apply=%region_2.3 | reduce | flops 3145728 | bytes 10485762 | tf_op jit(solution)/shard_map/reduce_sum | solution.py:32
  491.3 2.7 broadcast_in_dim.118
  494.1 81.4 %while.23 = (s32[]{:T(128)}, f32[1024,1024]{0,1:T(8,128)}, f32[1024,256]{0,1:T(8,128)S(1)}, s32[]{:T(128)}, s32[1024]{0:T(1024)S(1)}, /*index=5*/bf16[16,64,1024...) while((s32[]{:T(128)}, f32[1024,1024]{0,1:T(8,128)}, ...), condition=%wide.region_9.10_spmd, body=%wide.region_8.9_spmd.sunk | while | flops 170394624 | bytes 10919075 | solution.py:87
  496.3 0.6 broadcast_compare_fusion.5
  496.9 5.7 bitcast_add_fusion.2
  502.6 1.1 fusion.42
  507.7 5.0 bitcast_add_fusion.2
  512.6 1.1 fusion.42
  517.0 0.6 broadcast_compare_fusion.5
  517.6 5.0 bitcast_add_fusion.2
  522.6 1.1 fusion.42
  527.0 0.6 broadcast_compare_fusion.5
  527.6 5.0 bitcast_add_fusion.2
  532.6 1.1 fusion.42
  537.6 5.0 bitcast_add_fusion.2
  542.5 1.1 fusion.42
  547.5 5.0 bitcast_add_fusion.2
  552.5 1.1 fusion.42
  557.5 5.0 bitcast_add_fusion.2
  562.5 1.1 fusion.42
  567.5 5.1 bitcast_add_fusion.2
  572.6 1.1 fusion.42
  575.5 5.4 copy.25
  581.2 10.0 %all-gather.3.cloned.1.call-done = bf16[1024,8192]{1,0:T(8,128)(2,1)} async-done(((bf16[1024,2048]{1,0:T(8,128)(2,1)}), bf16[1024,8192]{1,0:T(8,128)(2,1)}) %all-gather.3.cloned.1.call-update) | async-done | bytes 16777232 | tf_op jit(solution)/shard_map/all_gather | solution.py:60
  591.2 24.8 %add_convert_fusion = bf16[1024,1024]{1,0:T(8,128)(2,1)} fusion(f32[1024,1024]{1,0:T(8,128)} %copy.25, bf16[1024,8192]{1,0:T(8,128)(2,1)} %all-gather.3.cloned.1.call-done, bf16[8192,1024]{1,0:T(8,128)(2,1)} %param.14), kind=kOutput, calls=%fused_computation.23 | convolution fusion | flops 17183014912 | bytes 39845888 | tf_op jit(solution)/shard_map/dot_general | solution.py:61
  616.1 5.3 fusion.14
  (44 shorter events, 4.3 us)
Async XLA Ops:
  7.2 9.6 %copy-start = (bf16[64,64,256]{2,1,0:T(8,128)(2,1)S(1)}, bf16[64,64,256]{2,1,0:T(8,128)(2,1)}, u32[]{:S(2)}) copy-start(bf16[64,64,256]{2,1,0:T(8,128)(2,1)} %param.18) | copy-start | bytes 6291460
  7.2 326.6 %all-reduce.4.cloned.1.call-start = ((), (), s32[]{:S(2)}) async-start(), calls=%async_computation.2 | async-start | bytes 17825792 | tf_op jit(solution)/shard_map/psum | solution.py:48
  25.9 457.9 %all-gather.5.cloned.1.call-start = ((), (), s32[]{:S(2)}) async-start(), calls=%async_computation.1 | async-start | bytes 10485760 | tf_op jit(solution)/shard_map/all_gather | solution.py:31
  31.6 0.8 copy-start.2
  31.6 559.6 %all-gather.3.cloned.1.call-start = ((), (), s32[]{:S(2)}) async-start(), calls=%async_computation | async-start | bytes 20971520 | tf_op jit(solution)/shard_map/all_gather | solution.py:60
  591.2 24.8 %copy-start.3 = (bf16[1024,8192]{1,0:T(8,128)(2,1)S(1)}, bf16[1024,8192]{1,0:T(8,128)(2,1)}, u32[]{:S(2)}) copy-start(bf16[1024,8192]{1,0:T(8,128)(2,1)} %all-gather.3.cloned.1.call-done) | copy-start | bytes 50331652
  591.2 24.8 %copy-start.4 = (bf16[8192,256]{1,0:T(8,128)(2,1)S(1)}, bf16[8192,256]{1,0:T(8,128)(2,1)}, u32[]{:S(2)}) copy-start(bf16[8192,256]{1,0:T(8,128)(2,1)} %param.15) | copy-start | bytes 12582916
  616.1 5.3 copy-start.1
Sparse Core Ops, SparseCore 0:
  26.0 307.7 all-reduce.3
  335.9 147.7 all-gather.4
  485.3 105.8 all-gather.2
